TPU v7x, 128 devices: a whole 4x4x4 slice. The times are simulated.
128 devices in a mesh: tile: 64 (over z, y, x), slide: 2 (over core).
Axes of the slice: x: 4, y: 4, z: 4, core: 2. Of those that a mesh axis runs over, the one named last changes fastest.
Arguments:
- features: bfloat16 [256, 32, 32, 256], P(('slide', 'tile')), parts along dimension 0, may hold values from -8 to 8
- neighbours: int32 [256, 8], P(('slide', 'tile')), parts along dimension 0, may hold values from 0 to 128, as said below
- conv_weight: bfloat16 [3, 3, 256, 256], replicated, may hold values from -0.125 to 0.125
- patch_weight: bfloat16 [4096, 768], replicated, may hold values from -1 to 1
- query_weight: bfloat16 [768, 768], replicated, may hold values from -2 to 2
- key_weight: bfloat16 [768, 768], replicated, may hold values from -2 to 2
- value_weight: bfloat16 [768, 768], replicated, may hold values from -0.21875 to 0.21875
- output_weight: bfloat16 [768, 768], replicated, may hold values from -0.21875 to 0.21875
- cotangent: bfloat16 [16384, 768], P(('slide', 'tile')), parts along dimension 0, may hold values from -6 to 6
Outputs:
- mixed: bfloat16 [16384, 768], P(('slide', 'tile')), parts along dimension 0
- output_grad: float32 [1536, 768], P('slide'), parts along dimension 0
There are 2 independent parts, one for each index of `slide`. A program takes and returns all parts, laid end to end along the dimension named above; an argument that names none is the same for every part. Nothing has to cross between parts.
Inputs may be any that keep to these rules, and one draw needn't show every extreme that they name: Tiles are tissue cells of a grid 16 cells wide; the tile numbers are given to the tissue cells in a drawn order, so neighbours may have any numbers; each entry is the index of the tissue tile at that grid offset, or 128.
All inputs are finite; a program needn't handle non-finite values.
Results may differ from a plain program's by a relative error of at most 0.02.
Values may be sent and summed in bfloat16 or wider, within the bound.
No kernel may reach another device: no remote copies, remote signals or barrier semaphores. Data moves between devices by JAX's collectives and lax.ppermute only.
A program may use at most 192 MiB of HBM per device.

v0:
```python
import jax
import jax.numpy as jnp
from jax import lax
from jax.sharding import PartitionSpec as P

PATCH = 4
HEADS = 12
HD = 64


def tile_faces(maps):
    return jnp.stack([maps[:, 0], maps[:, -1], maps[:, :, 0], maps[:, :, -1]], axis=1)


def pad_tiles(maps, all_faces, links):
    upper = all_faces[links[:, 1], 1]
    lower = all_faces[links[:, 6], 0]
    left_col = all_faces[links[:, 3], 3]
    right_col = all_faces[links[:, 4], 2]
    corner_ul = all_faces[links[:, 0], 1, -1]
    corner_ur = all_faces[links[:, 2], 1, 0]
    corner_dl = all_faces[links[:, 5], 0, -1]
    corner_dr = all_faces[links[:, 7], 0, 0]
    top_row = jnp.concatenate([corner_ul[:, None], upper, corner_ur[:, None]], axis=1)
    bottom_row = jnp.concatenate([corner_dl[:, None], lower, corner_dr[:, None]], axis=1)
    middle = jnp.concatenate([left_col[:, :, None], maps, right_col[:, :, None]], axis=2)
    return jnp.concatenate([top_row[:, None], middle, bottom_row[:, None]], axis=1)


def conv_tiles(padded, kernel):
    count = padded.shape[0]
    side = padded.shape[1] - 2
    chans = padded.shape[3]
    total = jnp.zeros((count * side * side, kernel.shape[3]), jnp.float32)
    for row_off in range(3):
        for col_off in range(3):
            window = padded[:, row_off : row_off + side, col_off : col_off + side, :].reshape(
                -1, chans
            )
            total = total + jnp.dot(
                window, kernel[row_off, col_off], preferred_element_type=jnp.float32
            )
    return jax.nn.gelu(total).astype(jnp.bfloat16).reshape(count, side, side, -1)


def patchify(hidden, patch):
    count, side, _, chans = hidden.shape
    blocks = side // patch
    grid = hidden.reshape(count, blocks, patch, blocks, patch, chans).transpose(0, 1, 3, 2, 4, 5)
    return grid.reshape(count * blocks * blocks, patch * patch * chans)


def local(
    features,
    neighbours,
    conv_weight,
    patch_weight,
    query_weight,
    key_weight,
    value_weight,
    output_weight,
    cotangent,
):
    local_faces = tile_faces(features)
    gathered = lax.all_gather(local_faces, "tile", axis=0, tiled=True)
    all_faces = jnp.concatenate(
        [gathered, jnp.zeros((1,) + gathered.shape[1:], jnp.bfloat16)], axis=0
    )
    padded = pad_tiles(features, all_faces, neighbours)
    hidden = conv_tiles(padded, conv_weight)
    tokens = jnp.dot(
        patchify(hidden, PATCH), patch_weight, preferred_element_type=jnp.float32
    ).astype(jnp.bfloat16)
    rows = tokens.shape[0]
    query = (
        jnp.dot(tokens, query_weight, preferred_element_type=jnp.float32)
        .astype(jnp.bfloat16)
        .reshape(rows, HEADS, HD)
    )
    scale = HD ** (-0.5)
    keys = jnp.dot(tokens, key_weight, preferred_element_type=jnp.float32).astype(jnp.bfloat16)
    values = jnp.dot(tokens, value_weight, preferred_element_type=jnp.float32).astype(jnp.bfloat16)
    top = jnp.full((HEADS, rows), -1e30, jnp.float32)
    key_heads = lax.all_gather(keys, "tile", axis=0, tiled=True).reshape(-1, HEADS, HD)
    value_heads = lax.all_gather(values, "tile", axis=0, tiled=True).reshape(-1, HEADS, HD)
    scores = (
        jnp.einsum("qhd,khd->hqk", query, key_heads, preferred_element_type=jnp.float32) * scale
    )
    new_top = jnp.maximum(top, jnp.max(scores, axis=-1))
    weights = jnp.exp(scores - new_top[..., None])
    total = jnp.sum(weights, axis=-1)
    accum = jnp.einsum(
        "hqk,khd->hqd",
        weights.astype(jnp.bfloat16),
        value_heads,
        preferred_element_type=jnp.float32,
    )
    top, total, accum = (new_top, total, accum)
    attended = (
        (accum / total[..., None]).transpose(1, 0, 2).reshape(rows, HEADS * HD).astype(jnp.bfloat16)
    )
    mixed = (
        tokens.astype(jnp.float32)
        + jnp.dot(attended, output_weight, preferred_element_type=jnp.float32)
    ).astype(jnp.bfloat16)
    grad_term = jnp.dot(attended.T, cotangent, preferred_element_type=jnp.float32)
    output_grad = lax.psum(grad_term, "tile")
    return (mixed, output_grad)


def solution(mesh):
    in_specs = (
        P(("slide", "tile"), None, None, None),
        P(("slide", "tile"), None),
        P(),
        P(),
        P(),
        P(),
        P(),
        P(),
        P(("slide", "tile"), None),
    )
    out_specs = (P(("slide", "tile"), None), P("slide", None))
    return jax.shard_map(local, mesh=mesh, in_specs=in_specs, out_specs=out_specs, check_vma=False)
```

profile of v0, /device:TPU:0, one launch (start us, length us, event | category | flops | bytes accessed | tf_op | source)
XLA Modules:
  0.0 506.7 jit_solution(2070060483644725372)
XLA Ops:
  7.2 1.2 fusion.78
  8.5 0.8 fusion.77
  9.3 0.7 pad_maximum_fusion.3
  10.0 1.3 fusion.68
  11.3 81.0 %all-gather.4.cloned.1.call-done = bf16[128,4,32,256]{3,2,1,0:T(8,128)(2,1)} async-done(((bf16[2,4,32,256]{3,2,1,0:T(8,128)(2,1)}), bf16[128,4,32,256]{3,2,1,0:T(8,128)(2,1)}) %all-gather.4.cloned.1.call-update) | async-done | bytes 8388624 | tf_op jit(solution)/shard_map/all_gather | solution.py:65
  92.3 8.5 %concatenate.53 = bf16[129,4,32,256]{3,2,1,0:T(8,128)(2,1)} pad(bf16[128,4,32,256]{3,2,1,0:T(8,128)(2,1)} %all-gather.4.cloned.1.call-done, bf16[]{:T(256)} %constant.15.clone.1), padding=0_1x0_0x0_0x0_0 | pad | bytes 16842754 | tf_op jit(solution)/shard_map/concatenate | solution.py:66
  100.8 3.9 gather_fusion.1
  104.8 1.5 gather_fusion
  106.3 1.5 gather_fusion.2
  107.8 3.9 gather_fusion.6
  111.7 1.5 gather_fusion.5
  113.2 1.5 gather_fusion.7
  114.7 3.9 gather_fusion.3
  118.7 4.0 gather_fusion.4
  122.7 1.2 pad_maximum_fusion.1
  124.0 1.7 pad_maximum_fusion
  125.7 0.8 fusion.76
  126.5 0.8 fusion.75
  127.2 0.5 copy-done.5
  127.7 0.4 fusion.32
  128.2 0.4 convolution_add_fusion.7
  128.6 0.4 convolution_add_fusion.6
  129.1 0.4 convolution_add_fusion.5
  129.5 0.4 convolution_add_fusion.4
  129.9 0.4 convolution_add_fusion.3
  130.4 0.4 convolution_add_fusion.2
  130.8 0.5 convolution_add_fusion.1
  131.3 0.9 fusion.13
  132.2 0.3 reshape_reshape.3
  132.5 0.4 copy.60
  132.9 0.8 reshape.58
  133.7 3.8 convolution_convert_fusion.3
  137.5 1.0 convolution_convert_fusion.1
  138.6 2.3 convolution_convert_fusion
  140.9 0.2 all-reduce.8.cloned.1.call-start
  141.2 0.3 convolution_convert_fusion.2
  141.5 0.2 copy.52
  141.7 87.6 %all-gather.6.cloned.1.call-done = bf16[8192,768]{1,0:T(8,128)(2,1)} async-done(((bf16[128,768]{1,0:T(8,128)(2,1)}), bf16[8192,768]{1,0:T(8,128)(2,1)}) %all-gather.6.cloned.1.call-update) | async-done | bytes 12582928 | tf_op jit(solution)/shard_map/all_gather | solution.py:84
  229.2 15.8 %copy.53 = bf16[8192,768]{0,1:T(8,128)(2,1)} copy(bf16[8192,768]{1,0:T(8,128)(2,1)} %all-gather.6.cloned.1.call-done) | data formatting | bytes 25165824 | tf_op jit(solution)/shard_map/all_gather | solution.py:84
  245.0 22.0 %multiply_reduce_fusion = (f32[12,128]{1,0:T(8,128)S(1)}, f32[12,128,8192]{2,1,0:T(8,128)}) fusion(bf16[128,12,64]{0,2,1:T(8,128)(2,1)S(1)} %bitcast.106, bf16[8192,12,64]{0,2,1:T(8,128)(2,1)} %bitcast.92), kind=kOutput, calls=%fused_computation.9 | convolution fusion | flops 1635777024 | bytes 63117312 | tf_op jit(solution)/shard_map/qhd,khd->hqk/dot_general | solution.py:87
  267.0 21.7 %fusion = f32[12,128]{1,0:T(8,128)S(1)} fusion(f32[12,128,8192]{2,1,0:T(8,128)} %get-tuple-element.25, f32[12,128]{1,0:T(8,128)S(1)} %broadcast_maximum_fusion), kind=kLoop, calls=%fused_computation.10 | loop fusion | flops 37747200 | bytes 50343936 | tf_op jit(solution)/shard_map/reduce_sum | solution.py:91
  288.8 34.3 %all-gather.8.cloned.1.call-done = bf16[8192,768]{1,0:T(8,128)(2,1)} async-done(((bf16[128,768]{1,0:T(8,128)(2,1)}), bf16[8192,768]{1,0:T(8,128)(2,1)}) %all-gather.8.cloned.1.call-update) | async-done | bytes 12582928 | tf_op jit(solution)/shard_map/all_gather | solution.py:85
  323.1 15.8 %copy.54 = bf16[8192,768]{0,1:T(8,128)(2,1)} copy(bf16[8192,768]{1,0:T(8,128)(2,1)} %all-gather.8.cloned.1.call-done) | data formatting | bytes 25165824 | tf_op jit(solution)/shard_map/all_gather | solution.py:85
  338.9 22.2 %fusion.21 = bf16[128,12,64]{0,2,1:T(8,128)(2,1)S(1)} fusion(bf16[8192,12,64]{0,2,1:T(8,128)(2,1)} %bitcast.93, f32[12,128,8192]{2,1,0:T(8,128)} %get-tuple-element.25, f32[12,128]{1,0:T(8,128)S(1)} %broadcast_maximum_fusion, f32[128,12]{0,1:T(8,128)S(1)} %bitcast.109), kind=kOutput, calls=%fused_computation.42 | convolution fusion | flops 1648558080 | bytes 63123456 | tf_op jit(solution)/shard_map/hqk,khd->hqd/dot_general | solution.py:92
  361.1 1.9 fusion.79
  363.0 1.0 fusion.17
  364.1 132.8 %all-reduce.8.cloned.1.call-done = f32[768,768]{1,0:T(8,128)} async-done(((f32[768,768]{1,0:T(8,128)}), f32[768,768]{1,0:T(8,128)}) %all-reduce.8.cloned.1.call-update) | async-done | bytes 2359312 | tf_op jit(solution)/shard_map/psum | solution.py:107
  496.9 3.2 copy.62
  (30 shorter events, 0.4 us)
Async XLA Ops:
  7.2 130.3 %copy-start = (bf16[768,768]{1,0:T(8,128)(2,1)S(1)}, bf16[768,768]{1,0:T(8,128)(2,1)}, u32[]{:S(2)}) copy-start(bf16[768,768]{1,0:T(8,128)(2,1)} %param.14) | copy-start | bytes 3538948
  7.2 85.1 %all-gather.4.cloned.1.call-start = ((), (), s32[]{:S(2)}) async-start(), calls=%async_computation | async-start | bytes 8519680 | tf_op jit(solution)/shard_map/all_gather | solution.py:65
  10.0 219.3 %all-gather.6.cloned.1.call-start = ((), (), s32[]{:S(2)}) async-start(), calls=%async_computation.1 | async-start | bytes 12779520 | tf_op jit(solution)/shard_map/all_gather | solution.py:84
  11.3 111.4 %copy-start.2 = (bf16[2,32,32,256]{3,2,1,0:T(8,128)(2,1)S(1)}, bf16[2,32,32,256]{3,2,1,0:T(8,128)(2,1)}, u32[]{:S(2)}) copy-start(bf16[2,32,32,256]{3,2,1,0:T(8,128)(2,1)} %param.9) | copy-start | bytes 3145732
  126.5 1.3 copy-start.5
  137.5 3.6 copy-start.3
  138.6 184.5 %all-gather.8.cloned.1.call-start = ((), (), s32[]{:S(2)}) async-start(), calls=%async_computation.2 | async-start | bytes 12779520 | tf_op jit(solution)/shard_map/all_gather | solution.py:85
  140.9 356.0 %all-reduce.8.cloned.1.call-start = ((), (), s32[]{:S(2)}) async-start(), calls=%async_computation.3 | async-start | bytes 4718592 | tf_op jit(solution)/shard_map/psum | solution.py:107
  338.9 22.2 %copy-start.6 = (bf16[128,768]{1,0:T(8,128)(2,1)S(1)}, bf16[128,768]{1,0:T(8,128)(2,1)}, u32[]{:S(2)}) copy-start(bf16[128,768]{1,0:T(8,128)(2,1)} %param.17) | copy-start | bytes 589828
  361.1 1.9 copy-start.4
  363.0 137.1 %copy-start.1 = (bf16[768,768]{1,0:T(8,128)(2,1)S(1)}, bf16[768,768]{1,0:T(8,128)(2,1)}, u32[]{:S(2)}) copy-start(bf16[768,768]{1,0:T(8,128)(2,1)} %param.14) | copy-start | bytes 3538948
Sparse Core Ops, SparseCore 0:
  11.4 80.8 all-gather.3
  138.7 90.4 all-gather.5
  232.5 90.5 all-gather.7
  363.1 133.7 all-reduce.7
where the time goes:
time: 508 us; the launch traced here: 507 us
  waiting for transfers between devices  336 us (66%)
  local copies, waits for them, and re-layouts  70.9 us (14%)
  matrix products  58.9 us (12%)
  other arithmetic  26.6 us (5%)
  between operations  14 us (3%)
    psum x1, waiting for transfers between devices, local(): output_grad = lax.psum(grad_term, 'tile')  133 us
    all_gather x1, waiting for transfers between devices, local(): lax.all_gather(keys, 'tile', axis=0, tiled=True).reshape(-1, HEADS, HD)  87.6 us
    all_gather x1, waiting for transfers between devices, local(): gathered = lax.all_gather(local_faces, 'tile', axis=0, tiled=True)  81 us
    all_gather x1, waiting for transfers between devices, local(): lax.all_gather(values, 'tile', axis=0, tiled=True).reshape(-1, HEADS, HD)  34.3 us
    dot_general x1, matrix products, local(): jnp.einsum('hqk,khd->hqd', weights.astype(jnp.bfloat16), value_heads, pre...  22.2 us
    dot_general x1, matrix products, local(): jnp.einsum('qhd,khd->hqk', query, key_heads, preferred_element_type=jnp.f...  22 us
    reduce_sum x1, other arithmetic, local(): total = jnp.sum(weights, axis=-1)  21.7 us
    all_gather x1, local copies, waits for them, and re-layouts, local(): lax.all_gather(keys, 'tile', axis=0, tiled=True).reshape(-1, HEADS, HD)  15.8 us
  transfers between devices with their start and end apart: 4, of which 4 were waited for; matrix products, arithmetic and copies ran while one was open for 13% of the time, Pallas kernels for 0%

commit v1 on v0

--- a/solution.py
+++ b/solution.py
@@ -104,7 +104,8 @@
         + jnp.dot(attended, output_weight, preferred_element_type=jnp.float32)
     ).astype(jnp.bfloat16)
     grad_term = jnp.dot(attended.T, cotangent, preferred_element_type=jnp.float32)
-    output_grad = lax.psum(grad_term, "tile")
+    response = lax.all_gather(grad_term, "tile")
+    output_grad = jnp.sum(response, axis=0)
     return (mixed, output_grad)
 
 

time: 508 us -> 990 us (1.95)
  waiting for transfers between devices: 336 us -> 774 us
  other arithmetic: 26.6 us -> 73.6 us
    all_gather x0 -> x1, waiting for transfers between devices: none -> 571 us  [local(): response = lax.all_gather(grad_term, 'tile')]
    psum x1 -> x0, waiting for transfers between devices: 133 us -> none  [local(): output_grad = lax.psum(grad_term, 'tile')]
    reduce_sum x0 -> x1, other arithmetic: none -> 47 us  [local(): output_grad = jnp.sum(response, axis=0)]
  transfers between devices with their start and end apart: 4 -> 4, of which waited for: 4 -> 4; matrix products, arithmetic and copies ran while one was open for 13% -> 7% of each run, Pallas kernels for 0% -> 0%
where the time goes in v1:
time: 990 us; the launch traced here: 988 us
  waiting for transfers between devices  774 us (78%)
  other arithmetic  73.6 us (7%)
  local copies, waits for them, and re-layouts  67.7 us (7%)
  matrix products  58.9 us (6%)
  between operations  14.1 us (1%)
    all_gather x1, waiting for transfers between devices, local(): response = lax.all_gather(grad_term, 'tile')  571 us
    all_gather x1, waiting for transfers between devices, local(): lax.all_gather(keys, 'tile', axis=0, tiled=True).reshape(-1, HEADS, HD)  87.5 us
    all_gather x1, waiting for transfers between devices, local(): gathered = lax.all_gather(local_faces, 'tile', axis=0, tiled=True)  81 us
    reduce_sum x1, other arithmetic, local(): output_grad = jnp.sum(response, axis=0)  47 us
    all_gather x1, waiting for transfers between devices, local(): lax.all_gather(values, 'tile', axis=0, tiled=True).reshape(-1, HEADS, HD)  34.3 us
    dot_general x1, matrix products, local(): jnp.einsum('hqk,khd->hqd', weights.astype(jnp.bfloat16), value_heads, pre...  22.2 us
    dot_general x1, matrix products, local(): jnp.einsum('qhd,khd->hqk', query, key_heads, preferred_element_type=jnp.f...  22 us
    reduce_sum x1, other arithmetic, local(): total = jnp.sum(weights, axis=-1)  21.7 us
  transfers between devices with their start and end apart: 4, of which 4 were waited for; matrix products, arithmetic and copies ran while one was open for 7% of the time, Pallas kernels for 0%

profile of v1, /device:TPU:0, one launch (start us, length us, event | category | flops | bytes accessed | tf_op | source)
XLA Modules:
  0.0 988.2 jit_solution(14102967267242529243)
XLA Ops:
  7.2 0.9 fusion.77
  8.1 1.1 fusion.78
  9.3 0.7 pad_maximum_fusion.3
  10.0 1.3 fusion.68
  11.3 81.0 %all-gather.6.cloned.1.call-done = bf16[128,4,32,256]{3,2,1,0:T(8,128)(2,1)} async-done(((bf16[2,4,32,256]{3,2,1,0:T(8,128)(2,1)}), bf16[128,4,32,256]{3,2,1,0:T(8,128)(2,1)}) %all-gather.6.cloned.1.call-update) | async-done | bytes 8388624 | tf_op jit(solution)/shard_map/all_gather | solution.py:65
  92.3 8.5 concatenate.53
  100.8 1.5 gather_fusion.7
  102.3 1.5 gather_fusion.5
  103.8 1.5 gather_fusion.2
  105.3 1.5 gather_fusion
  106.8 4.0 gather_fusion.6
  110.7 4.0 gather_fusion.4
  114.7 4.0 gather_fusion.3
  118.6 4.0 gather_fusion.1
  122.7 1.2 pad_maximum_fusion.1
  124.0 1.7 pad_maximum_fusion
  125.7 0.8 fusion.75
  126.5 0.8 fusion.76
  127.3 0.5 copy-done.5
  127.7 0.4 fusion.32
  128.2 0.4 convolution_add_fusion.7
  128.6 0.4 convolution_add_fusion.6
  129.1 0.4 convolution_add_fusion.5
  129.5 0.4 convolution_add_fusion.4
  130.0 0.4 convolution_add_fusion.3
  130.4 0.4 convolution_add_fusion.2
  130.8 0.4 convolution_add_fusion.1
  131.3 0.9 fusion.13
  132.2 0.3 reshape_reshape.3
  132.5 0.4 copy.60
  132.9 0.8 reshape.58
  133.7 3.8 convolution_convert_fusion.3
  137.5 1.0 convolution_convert_fusion.1
  138.6 2.3 convolution_convert_fusion
  140.9 0.2 all-gather.12.cloned.1.call-start
  141.2 0.3 convolution_convert_fusion.2
  141.5 0.2 copy.52
  141.7 87.5 %all-gather.8.cloned.1.call-done = bf16[8192,768]{1,0:T(8,128)(2,1)} async-done(((bf16[128,768]{1,0:T(8,128)(2,1)}), bf16[8192,768]{1,0:T(8,128)(2,1)}) %all-gather.8.cloned.1.call-update) | async-done | bytes 12582928 | tf_op jit(solution)/shard_map/all_gather | solution.py:84
  229.2 15.8 %copy.53 = bf16[8192,768]{0,1:T(8,128)(2,1)} copy(bf16[8192,768]{1,0:T(8,128)(2,1)} %all-gather.8.cloned.1.call-done) | data formatting | bytes 25165824 | tf_op jit(solution)/shard_map/all_gather | solution.py:84
  245.0 22.0 %multiply_reduce_fusion = (f32[12,128]{1,0:T(8,128)S(1)}, f32[12,128,8192]{2,1,0:T(8,128)}) fusion(bf16[128,12,64]{0,2,1:T(8,128)(2,1)S(1)} %bitcast.107, bf16[8192,12,64]{0,2,1:T(8,128)(2,1)} %bitcast.93), kind=kOutput, calls=%fused_computation.9 | convolution fusion | flops 1635777024 | bytes 63117312 | tf_op jit(solution)/shard_map/qhd,khd->hqk/dot_general | solution.py:87
  267.0 21.7 %fusion = f32[12,128]{1,0:T(8,128)S(1)} fusion(f32[12,128,8192]{2,1,0:T(8,128)} %get-tuple-element.25, f32[12,128]{1,0:T(8,128)S(1)} %broadcast_maximum_fusion), kind=kLoop, calls=%fused_computation.10 | loop fusion | flops 37747200 | bytes 50343936 | tf_op jit(solution)/shard_map/reduce_sum | solution.py:91
  288.8 34.3 %all-gather.10.cloned.1.call-done = bf16[8192,768]{1,0:T(8,128)(2,1)} async-done(((bf16[128,768]{1,0:T(8,128)(2,1)}), bf16[8192,768]{1,0:T(8,128)(2,1)}) %all-gather.10.cloned.1.call-update) | async-done | bytes 12582928 | tf_op jit(solution)/shard_map/all_gather | solution.py:85
  323.1 15.8 %copy.54 = bf16[8192,768]{0,1:T(8,128)(2,1)} copy(bf16[8192,768]{1,0:T(8,128)(2,1)} %all-gather.10.cloned.1.call-done) | data formatting | bytes 25165824 | tf_op jit(solution)/shard_map/all_gather | solution.py:85
  338.8 22.2 %fusion.21 = bf16[128,12,64]{0,2,1:T(8,128)(2,1)S(1)} fusion(bf16[8192,12,64]{0,2,1:T(8,128)(2,1)} %bitcast.94, f32[12,128,8192]{2,1,0:T(8,128)} %get-tuple-element.25, f32[12,128]{1,0:T(8,128)S(1)} %broadcast_maximum_fusion, f32[128,12]{0,1:T(8,128)S(1)} %bitcast.110), kind=kOutput, calls=%fused_computation.42 | convolution fusion | flops 1648558080 | bytes 63123456 | tf_op jit(solution)/shard_map/hqk,khd->hqd/dot_general | solution.py:92
  361.1 1.9 fusion.79
  363.0 1.0 fusion.17
  364.0 570.6 %all-gather.12.cloned.1.call-done = f32[49152,768]{1,0:T(8,128)} async-done(((f32[768,768]{1,0:T(8,128)}), f32[49152,768]{1,0:T(8,128)}) %all-gather.12.cloned.1.call-update) | async-done | bytes 150994960 | tf_op jit(solution)/shard_map/all_gather | solution.py:107
  934.7 47.0 %reduce_sum.19 = f32[768,768]{1,0:T(8,128)} reduce(f32[64,768,768]{2,1,0:T(8,128)} %bitcast.37, f32[]{:T(128)} %constant.12.clone.1), dimensions={0}, to_apply=%region_2.0 | reduce | flops 37158912 | bytes 153354240 | tf_op jit(solution)/shard_map/reduce_sum | solution.py:108
  (30 shorter events, 0.4 us)
Async XLA Ops:
  7.2 130.4 %copy-start = (bf16[768,768]{1,0:T(8,128)(2,1)S(1)}, bf16[768,768]{1,0:T(8,128)(2,1)}, u32[]{:S(2)}) copy-start(bf16[768,768]{1,0:T(8,128)(2,1)} %param.14) | copy-start | bytes 3538948
  7.2 85.1 %all-gather.6.cloned.1.call-start = ((), (), s32[]{:S(2)}) async-start(), calls=%async_computation | async-start | bytes 8519680 | tf_op jit(solution)/shard_map/all_gather | solution.py:65
  10.0 219.2 %all-gather.8.cloned.1.call-start = ((), (), s32[]{:S(2)}) async-start(), calls=%async_computation.1 | async-start | bytes 12779520 | tf_op jit(solution)/shard_map/all_gather | solution.py:84
  11.3 111.5 %copy-start.2 = (bf16[2,32,32,256]{3,2,1,0:T(8,128)(2,1)S(1)}, bf16[2,32,32,256]{3,2,1,0:T(8,128)(2,1)}, u32[]{:S(2)}) copy-start(bf16[2,32,32,256]{3,2,1,0:T(8,128)(2,1)} %param.9) | copy-start | bytes 3145732
  126.5 1.3 copy-start.5
  137.5 3.6 copy-start.3
  138.6 184.5 %all-gather.10.cloned.1.call-start = ((), (), s32[]{:S(2)}) async-start(), calls=%async_computation.2 | async-start | bytes 12779520 | tf_op jit(solution)/shard_map/all_gather | solution.py:85
  140.9 793.7 %all-gather.12.cloned.1.call-start = ((), (), s32[]{:S(2)}) async-start(), calls=%async_computation.3 | async-start | bytes 153354240 | tf_op jit(solution)/shard_map/all_gather | solution.py:107
  338.8 22.2 %copy-start.6 = (bf16[128,768]{1,0:T(8,128)(2,1)S(1)}, bf16[128,768]{1,0:T(8,128)(2,1)}, u32[]{:S(2)}) copy-start(bf16[128,768]{1,0:T(8,128)(2,1)} %param.17) | copy-start | bytes 589828
  361.1 1.9 copy-start.4
  934.7 47.0 %copy-start.1 = (bf16[768,768]{1,0:T(8,128)(2,1)S(1)}, bf16[768,768]{1,0:T(8,128)(2,1)}, u32[]{:S(2)}) copy-start(bf16[768,768]{1,0:T(8,128)(2,1)} %param.14) | copy-start | bytes 3538948
Sparse Core Ops, SparseCore 0:
  11.4 80.8 all-gather.5
  138.7 90.4 all-gather.7
  232.5 90.5 all-gather.9
  363.1 571.5 all-gather.11
